TPU v7x, 256 devices: a whole 4x4x8 slice. The times are simulated.
256 devices in a mesh: bus: 64 (over z, y, core), tm: 4 (over x).
Axes of the slice: x: 4, y: 4, z: 8, core: 2. Of those that a mesh axis runs over, the one named last changes fastest.
Arguments:
- features: bfloat16 [8192, 64, 128], P('bus', 'tm'), may hold values from -6 to 6
- couplings: bfloat16 [128, 8, 64, 64], P('bus'), may hold values from -0.25 to 0.25
- neighbors: int32 [128, 8], P('bus'), may hold values from 0 to 127, as said below
- w_graph: bfloat16 [128, 128], replicated, may hold values from -0.5 to 0.5
- kernel_taps: bfloat16 [64, 128], replicated, may hold values from -0.3984375 to 0.3984375
- w_out: bfloat16 [128, 128], replicated, may hold values from -0.5 to 0.5
- cotangent: bfloat16 [8192, 64, 128], P('bus', 'tm'), may hold values from -6 to 6
Outputs:
- grad_features: bfloat16 [8192, 64, 128], P('bus', 'tm')
- grad_graph: float32 [128, 128], replicated
- grad_out: float32 [128, 128], replicated
- grad_taps: float32 [64, 128], replicated
Inputs may be any that keep to these rules, and one draw needn't show every extreme that they name: neighbors[i, 0] = i. Counting 2 blocks to each index of bus, every entry of block i names a block of the same index, one of the last 1 block of the index before, or one of the first 1 block of the index after.
All inputs are finite; a program needn't handle non-finite values.
Results may differ from a plain program's by a relative error of at most 0.0067.
Values may be sent and summed in bfloat16 or wider, within the bound.
A program may use at most 64 MiB of HBM per device.

v0:
```python
import math

import jax
import jax.numpy as jnp
from jax import lax
from jax.sharding import PartitionSpec as P


def with_halo(array, sides, width):
    for axis, dim in sides:
        size, length = (lax.axis_size(axis), array.shape[dim])
        up = [(i, (i + 1) % size) for i in range(size - 1)]
        down = [(j, i) for i, j in up]
        last = lax.slice_in_dim(array, length - width, length, axis=dim)
        first = lax.slice_in_dim(array, 0, width, axis=dim)
        before = lax.ppermute(last, axis, up)
        after = lax.ppermute(first, axis, down)
        array = jnp.concatenate([before, array, after], axis=dim)
    return array


def shifted(value, axis, steps):
    count = lax.axis_size(axis)
    first, last = (max(0, -steps), min(count, count - steps))
    return lax.ppermute(value, axis, [(source, source + steps) for source in range(first, last)])


def toeplitz_table(kernel_taps):
    length = kernel_taps.shape[0]
    row_ids = jnp.arange(length, dtype=jnp.int32)
    lagged = row_ids[:, None] - row_ids[None, :]
    picked = jnp.take(kernel_taps.T, jnp.clip(lagged, 0, length - 1), axis=1)
    return jnp.where(lagged[None] >= 0, picked, jnp.zeros_like(picked))


def lag_sums(lag_table):
    channels = lag_table.shape[0]
    length = lag_table.shape[1]
    flipped = lag_table[:, :, ::-1]
    padded = jnp.pad(flipped, ((0, 0), (0, 0), (0, 1)))
    flat_view = padded.reshape(channels, length * (length + 1))
    window = flat_view[:, length - 1 : length - 1 + length * length].reshape(
        channels, length, length
    )
    row_ids = jnp.arange(length, dtype=jnp.int32)
    lag_mask = row_ids[None, :, None] >= row_ids[None, None, :]
    return jnp.sum(jnp.where(lag_mask, window, jnp.zeros_like(window)), axis=1).T


def silu_slope(pre_act):
    sigmoid_val = jax.nn.sigmoid(pre_act)
    return sigmoid_val * (1.0 + pre_act * (1.0 - sigmoid_val))


def shards(features, couplings, neighbors, w_graph, kernel_taps, w_out, cotangent):
    bus_rows, steps_per_shard, channels = features.shape
    blocks_dev = couplings.shape[0]
    slot_count = couplings.shape[1]
    block_rows = couplings.shape[2]
    flat_len = steps_per_shard * channels
    offset = neighbors - lax.axis_index("bus") * blocks_dev
    extended = with_halo(features, (("bus", 0),), blocks_dev * block_rows)
    position = offset + blocks_dev
    ext_blocks = extended.reshape(-1, block_rows, flat_len)
    picked = ext_blocks[position]
    mixed_blocks = jnp.einsum(
        "ikab,ikbn->ian", couplings, picked, preferred_element_type=jnp.float32
    ).astype(jnp.bfloat16)
    mixed_rows = mixed_blocks.reshape(bus_rows * steps_per_shard, channels)
    pre_act = jnp.dot(mixed_rows, w_graph, preferred_element_type=jnp.float32)
    activated = (
        jax.nn.silu(pre_act).astype(jnp.bfloat16).reshape(bus_rows, steps_per_shard, channels)
    )
    act_week, cot_week = (
        lax.all_to_all(activated, "tm", split_axis=0, concat_axis=1, tiled=True),
        lax.all_to_all(cotangent, "tm", split_axis=0, concat_axis=1, tiled=True),
    )
    lag_table = toeplitz_table(kernel_taps)
    convolved_rows = jnp.einsum(
        "cts,bsc->btc", lag_table, act_week, preferred_element_type=jnp.float32
    ).astype(jnp.bfloat16)
    part_out = jnp.einsum(
        "btc,btd->cd", convolved_rows, cot_week, preferred_element_type=jnp.float32
    )
    grad_conv = jnp.einsum(
        "btd,cd->btc", cot_week, w_out, preferred_element_type=jnp.float32
    ).astype(jnp.bfloat16)
    part_taps = lag_sums(
        jnp.einsum("btc,bsc->cts", grad_conv, act_week, preferred_element_type=jnp.float32)
    )
    grad_act = jnp.einsum(
        "cts,btc->bsc", lag_table, grad_conv, preferred_element_type=jnp.float32
    ).astype(jnp.bfloat16)
    grad_back = lax.all_to_all(grad_act, "tm", split_axis=1, concat_axis=0, tiled=True)
    grad_pre = (grad_back.reshape(-1, channels).astype(jnp.float32) * silu_slope(pre_act)).astype(
        jnp.bfloat16
    )
    part_graph = lax.dot_general(
        mixed_rows, grad_pre, (((0,), (0,)), ((), ())), preferred_element_type=jnp.float32
    )
    grad_mixed = lax.dot_general(
        grad_pre, w_graph, (((1,), (1,)), ((), ())), preferred_element_type=jnp.float32
    )
    grad_mixed = grad_mixed.astype(jnp.bfloat16).reshape(blocks_dev, block_rows, flat_len)
    spread = jnp.zeros((blocks_dev + 2 * blocks_dev, block_rows, flat_len), jnp.float32)
    for slot_index in range(slot_count):
        slot_term = jnp.einsum(
            "iab,ian->ibn", couplings[:, slot_index], grad_mixed, preferred_element_type=jnp.float32
        )
        spread = spread.at[position[:, slot_index]].add(slot_term)
    own_part = spread[blocks_dev : blocks_dev + blocks_dev]
    before = spread[:blocks_dev]
    after_part = spread[blocks_dev + blocks_dev :]
    from_after = shifted(before.astype(jnp.bfloat16), "bus", -1).astype(before.dtype)
    from_before = shifted(after_part.astype(jnp.bfloat16), "bus", 1).astype(after_part.dtype)
    own_part = own_part.at[blocks_dev - blocks_dev :].add(from_after)
    own_part = own_part.at[:blocks_dev].add(from_before)
    grad_features = (
        own_part.reshape(bus_rows, steps_per_shard, channels) + cotangent.astype(jnp.float32)
    ).astype(jnp.bfloat16)
    summed = lax.psum((part_graph, part_out, part_taps), ("bus", "tm"))
    total_rows = (
        lax.axis_size("bus") * blocks_dev * block_rows * steps_per_shard * lax.axis_size("tm")
    )
    grad_scale = 1.0 / math.sqrt(total_rows)
    return (grad_features, summed[0] * grad_scale, summed[1] * grad_scale, summed[2] * grad_scale)


def solution(mesh):
    return jax.shard_map(
        shards,
        mesh=mesh,
        in_specs=(
            P("bus", "tm", None),
            P("bus", None, None, None),
            P("bus", None),
            P(),
            P(),
            P(),
            P("bus", "tm", None),
        ),
        out_specs=(P("bus", "tm", None), P(), P(), P()),
        check_vma=False,
    )
```

profile of v0, /device:TPU:1, one launch (start us, length us, event | category | flops | bytes accessed | tf_op | source)
XLA Modules:
  0.0 479.4 jit_solution(11874590185701983800)
XLA Ops:
  7.2 4.7 collective-permute-start
  11.9 1.9 collective-permute-start.1
  13.8 4.0 all-to-all-start
  18.8 12.1 %gather_fusion = bf16[4096,128]{1,0:T(8,128)(2,1)S(1)} fusion(bf16[128,64]{0,1:T(8,128)(2,1)S(1)} %bitcast.131, s32[4096]{0:T(1024)S(1)} %broadcast_clamp_fusion), kind=kCustom, calls=%fused_computation | custom fusion | bytes 2113536 | tf_op jit(solution)/shard_map/jit(_take)/gather | solution.py:32
  30.9 3.8 copy.61
  37.8 2.6 fusion.15
  40.5 2.3 copy.63
  42.8 4.3 all-to-all-start.1
  50.3 2.7 gather_fusion.1
  53.0 3.1 fusion.1
  71.1 2.2 scatter_fusion
  73.3 2.1 scatter_fusion.1
  75.5 2.2 scatter_fusion.2
  77.6 2.2 scatter_fusion.3
  79.8 2.2 scatter_fusion.4
  82.0 2.2 scatter_fusion.5
  84.2 2.2 scatter_fusion.6
  86.4 2.2 scatter_fusion.7
  89.9 4.1 all-to-all-start.2
  94.2 2.5 fusion.59
  96.6 2.2 collective-permute-start.2
  98.8 4.8 collective-permute-start.3
  106.5 3.3 copy.75
  109.9 3.2 fusion.12
  113.1 2.7 fusion.61
  117.3 7.2 %rev.3 = f32[128,64,64]{2,1,0:T(8,128)} reverse(f32[128,64,64]{2,1,0:T(8,128)} %fusion.61), dimensions={2} | reverse | bytes 4194304 | tf_op jit(solution)/shard_map/rev | solution.py:39
  124.5 4.9 %pad.10 = f32[128,64,65]{2,1,0:T(8,128)} pad(f32[128,64,64]{2,1,0:T(8,128)} %rev.3, f32[]{:T(128)} %constant.102.clone.1), padding=0_0x0_0x0_1 | pad | bytes 4227076 | tf_op jit(solution)/shard_map/jit(_pad)/pad | solution.py:40
  129.5 5.1 %reshape.265 = f32[128,4160]{1,0:T(8,128)} reshape(f32[128,64,65]{2,1,0:T(8,128)} %pad.10) | data formatting | bytes 4259840 | tf_op jit(solution)/shard_map/reshape | solution.py:41
  134.5 3.6 slice.127
  138.1 2.9 copy.90
  142.9 83.5 %psum.23 = f32[64,128]{1,0:T(8,128)S(1)} all-reduce(f32[64,128]{1,0:T(8,128)S(1)} %bitcast.142), channel_id=1, replica_groups=mesh['bus'=64,'tm'=4] {'bus','tm'}, use_global_device_ids=true, to_apply=%region_11.12 | all-reduce | flops 8192 | bytes 65536 | tf_op jit(solution)/shard_map/psum | solution.py:121
  227.1 240.0 %all-reduce.4.cloned.1.call-done = (f32[128,128]{1,0:T(8,128)}, f32[128,128]{1,0:T(8,128)}) async-done(((f32[128,128]{1,0:T(8,128)}, f32[128,128]{1,0:T(8,128)}), (f32[128,128]{1,0:T(8,128)}, f32[128,128]{1,0:T(8,128)})) %all-reduce.4.cloned.1.call-update) | async-done | bytes 131088 | tf_op jit(solution)/shard_map/psum | solution.py:121
  (80 shorter events, 35.8 us)
Async XLA Ops:
  7.2 51.0 %copy-start = (bf16[128,128]{1,0:T(8,128)(2,1)S(1)}, bf16[128,128]{1,0:T(8,128)(2,1)}, u32[]{:S(2)}) copy-start(bf16[128,128]{1,0:T(8,128)(2,1)} %param.18) | copy-start | bytes 98308
  7.2 11.6 %copy-start.1 = (bf16[64,128]{1,0:T(8,128)(2,1)S(1)}, bf16[64,128]{1,0:T(8,128)(2,1)}, u32[]{:S(2)}) copy-start(bf16[64,128]{1,0:T(8,128)(2,1)} %param.19) | copy-start | bytes 49156
  7.2 39.9 %collective-permute-start = (bf16[128,16,128]{2,1,0:T(8,128)(2,1)}, bf16[128,16,128]{2,1,0:T(8,128)(2,1)S(1)}, u32[]{:S(2)}, u32[]{:S(2)}) collective-permute-start(bf16[128,16,128]{2,1,0:T(8,128)(2,1)} %param.15), channel_id=1, source_target_pairs={{0,4},{4,8},{8,12},{12,16},{16,20},{20,24},{24,28},{28,32},{32,36}... | collective-permute-start | bytes 1572872 | tf_op jit(solution)/shard_map/ppermute | solution.py:16
  11.9 36.1 %collective-permute-start.1 = (bf16[128,16,128]{2,1,0:T(8,128)(2,1)}, bf16[128,16,128]{2,1,0:T(8,128)(2,1)}, u32[]{:S(2)}, u32[]{:S(2)}) collective-permute-start(bf16[128,16,128]{2,1,0:T(8,128)(2,1)} %param.15), channel_id=1, source_target_pairs={{4,0},{8,4},{12,8},{16,12},{20,16},{24,20},{28,24},{32,28},{36,32}... | collective-permute-start | bytes 1572872 | tf_op jit(solution)/shard_map/ppermute | solution.py:17
  13.8 21.2 %all-to-all-start = ((bf16[128,16,128]{2,1,0:T(8,128)(2,1)}), bf16[128,16,128]{2,1,0:T(8,128)(2,1)S(1)}, u32[]{:S(2)}, u32[]{:S(2)}) async-start(bf16[128,16,128]{2,1,0:T(8,128)(2,1)} %param.21), calls=%async_computation | async-start | bytes 1048576 | tf_op jit(solution)/shard_map/all_to_all | solution.py:76
  30.9 5.0 %copy-start.14 = (bf16[128,128]{1,0:T(8,128)(2,1)S(1)}, bf16[128,128]{1,0:T(8,128)(2,1)}, u32[]{:S(2)}) copy-start(bf16[128,128]{1,0:T(8,128)(2,1)} %param.20) | copy-start | bytes 98308
  35.1 0.8 copy-start.6
  37.8 2.7 copy-start.2
  42.8 13.9 %all-to-all-start.1 = ((bf16[32,64,128]{2,0,1:T(8,128)(2,1)}), bf16[32,64,128]{2,0,1:T(8,128)(2,1)}, u32[]{:S(2)}, u32[]{:S(2)}) async-start(bf16[32,64,128]{2,0,1:T(8,128)(2,1)} %copy.63), calls=%async_computation.1 | async-start | bytes 1048576 | tf_op jit(solution)/shard_map/all_to_all | solution.py:94
  47.1 0.8 copy-start.13
  50.3 2.8 copy-start.5
  56.3 1.8 copy-start.8
  59.6 3.2 copy-start.10
  89.9 14.7 %all-to-all-start.2 = ((bf16[128,16,128]{2,1,0:T(8,128)(2,1)}), bf16[128,16,128]{2,1,0:T(8,128)(2,1)}, u32[]{:S(2)}, u32[]{:S(2)}) async-start(bf16[128,16,128]{2,1,0:T(8,128)(2,1)} %bitcast.141), calls=%async_computation.2 | async-start | bytes 1048576 | tf_op jit(solution)/shard_map/all_to_all | solution.py:75
  94.1 373.0 %all-reduce.4.cloned.1.call-start = ((), (), s32[]{:S(2)}) async-start(), calls=%async_computation.3 | async-start | bytes 262144 | tf_op jit(solution)/shard_map/psum | solution.py:121
  94.1 9.5 %copy-start.9 = (bf16[2048,128]{1,0:T(8,128)(2,1)S(1)}, bf16[2048,128]{1,0:T(8,128)(2,1)}, u32[]{:S(2)}) copy-start(bf16[2048,128]{1,0:T(8,128)(2,1)} %copy-done.8) | copy-start | bytes 1572868
  94.1 9.5 %copy-start.11 = (bf16[2048,128]{1,0:T(8,128)(2,1)S(1)}, bf16[2048,128]{1,0:T(8,128)(2,1)}, u32[]{:S(2)}) copy-start(bf16[2048,128]{1,0:T(8,128)(2,1)} %copy-done.10) | copy-start | bytes 1572868
  96.6 373.4 %collective-permute-start.2 = (bf16[2,64,2048]{2,1,0:T(8,128)(2,1)}, bf16[2,64,2048]{2,1,0:T(8,128)(2,1)}, u32[]{:S(2)}, u32[]{:S(2)}) collective-permute-start(bf16[2,64,2048]{2,1,0:T(8,128)(2,1)} %get-tuple-element.54), channel_id=1, source_target_pairs={{4,0},{8,4},{12,8},{16,12},{20,16},{24,20},{28,24},{32,28},{36,32}... | collective-permute-start | bytes 1572872 | tf_op jit(solution)/shard_map/ppermute | solution.py:25
  98.8 371.2 %collective-permute-start.3 = (bf16[2,64,2048]{2,1,0:T(8,128)(2,1)}, bf16[2,64,2048]{2,1,0:T(8,128)(2,1)}, u32[]{:S(2)}, u32[]{:S(2)}) collective-permute-start(bf16[2,64,2048]{2,1,0:T(8,128)(2,1)} %get-tuple-element.55), channel_id=1, source_target_pairs={{0,4},{4,8},{8,12},{12,16},{16,20},{20,24},{24,28},{28,32},{32,36}... | collective-permute-start | bytes 1572872 | tf_op jit(solution)/shard_map/ppermute | solution.py:25
  109.9 3.3 copy-start.3
  109.9 3.3 copy-start.4
  113.1 2.7 copy-start.7
  470.0 1.6 copy-start.12
Sparse Core Ops, SparseCore 0:
  226.6 240.4 all-reduce.3
where the time goes:
time: 481 us; the launch traced here: 479 us
  waiting for transfers between devices  240 us (50%)
  blocking collectives  83.5 us (17%)
  local copies, waits for them, and re-layouts  58.9 us (12%)
  other arithmetic  29.2 us (6%)
  matrix products  26.7 us (6%)
  starting transfers between devices  26.2 us (5%)
  between operations  14.5 us (3%)
    psum x1, waiting for transfers between devices, shards(): summed = lax.psum((part_graph, part_out, part_taps), ('bus', 'tm'))  240 us
    psum x1, blocking collectives, shards(): summed = lax.psum((part_graph, part_out, part_taps), ('bus', 'tm'))  83.5 us
    scatter-add x8, other arithmetic, shards(): spread = spread.at[position[:, slot_index]].add(slot_term)  17.4 us
    gather x2, local copies, waits for them, and re-layouts, toeplitz_table(): picked = jnp.take(kernel_taps.T, jnp.clip(lagged, 0, length - 1), axis=1)  15.9 us
    dot_general x8, matrix products, shards(): jnp.einsum('iab,ian->ibn', couplings[:, slot_index], grad_mixed, preferre...  10.6 us
  transfers between devices with their start and end apart: 8, of which 2 were waited for; matrix products, arithmetic and copies ran while one was open for 16% of the time, Pallas kernels for 0%

commit v1 on v0

v1 whole, which is shorter than its diff:
```python
import functools
import math

import jax
import jax.numpy as jnp
import ml_dtypes
import numpy as np
from jax import lax
from jax.experimental import pallas as pl
from jax.experimental.pallas import tpu as pltpu
from jax.sharding import PartitionSpec as P

CORES = 2
CHIPS_Y = 4
MESH = pl.DeviceIdType.MESH
F32 = jnp.float32
BF16 = jnp.bfloat16


def dft_tables(length):
    freq = 2 * np.arange(length)[:, None] + 1
    angle = np.pi * freq * np.arange(length)[None, :] / (2 * length)
    forward = np.concatenate([np.cos(angle), -np.sin(angle)], axis=0)
    inverse = forward.T / length

    def parts(table):
        high = table.astype(ml_dtypes.bfloat16)
        low = (table - high.astype(np.float64)).astype(ml_dtypes.bfloat16)
        return high, low

    f_high, f_low = parts(forward)
    i_high, i_low = parts(inverse)
    return (
        np.concatenate([f_high, f_low], axis=1),
        np.concatenate([i_high, i_high, i_low], axis=1),
    )


def split(value):
    high = value.astype(BF16)
    low = (value - high.astype(F32)).astype(BF16)
    return high, low


def mm(a, b):
    return jnp.dot(a, b, preferred_element_type=F32)


def mm_t(a, b, da, db):
    return lax.dot_general(a, b, (((da,), (db,)), ((), ())), preferred_element_type=F32)


def kernel(
    sizes,
    feat,
    cot,
    coup,
    nbr,
    wg,
    taps,
    wo,
    fwd_tab,
    inv_tab,
    grad_feat,
    grad_graph,
    grad_out,
    grad_taps,
    fx,
    ft,
    perm,
    m_mat,
    mt_mat,
    mixed,
    slope,
    act_t,
    act_b,
    act_w,
    cot_v,
    cot_w,
    gc_w,
    g_freq,
    kr,
    ki,
    grad_w,
    grad_b,
    own,
    send_prev,
    send_next,
    from_prev,
    from_next,
    out_v,
    red_a,
    rs_a,
    y_a,
    z_a,
    sum_a,
    red_b,
    rs_b,
    y_b,
    z_b,
    sum_b,
    loc_sem,
    out_sem,
    halo_s,
    halo_r,
    cot_s,
    cot_r,
    act_s,
    act_r,
    grd_s,
    grd_r,
    ghalo_s,
    ghalo_r,
    rsa_s,
    rsa_r,
    rsb_s,
    rsb_r,
    ya_s,
    ya_r,
    yb_s,
    yb_r,
    za_s,
    za_r,
    zb_s,
    zb_r,
    aga_s,
    aga_r,
    agb_s,
    agb_r,
):
    nbus, nx, ny, nz, scale = sizes
    rows, steps, chans = feat.shape
    block = rows // 2
    share = rows // nx
    nq = nx * CORES
    bus = lax.axis_index("bus")
    tm = lax.axis_index("tm")
    core = lax.rem(bus, CORES)
    yy = lax.rem(bus // CORES, ny)
    zz = bus // (CORES * ny)
    qq = tm * CORES + core

    def dev_bus(step):
        return {"bus": lax.rem(bus + (nbus + step), nbus), "tm": tm}

    def dev_x(step):
        return {"bus": bus, "tm": lax.rem(tm + step, nx)}

    def q_at(step):
        return lax.rem(qq + step, nq)

    def dev_q(step):
        other = q_at(step)
        return {"bus": bus - core + lax.rem(other, CORES), "tm": other // CORES}

    def dev_y(step):
        return {"bus": (zz * ny + lax.rem(yy + step, ny)) * CORES + core, "tm": tm}

    def dev_z(step):
        return {"bus": (lax.rem(zz + step, nz) * ny + yy) * CORES + core, "tm": tm}

    def remote(src, dst, send, recv, device):
        return pltpu.make_async_remote_copy(
            src_ref=src, dst_ref=dst, send_sem=send, recv_sem=recv, device_id=device, device_id_type=MESH
        )

    copy_feat = pltpu.make_async_copy(feat, fx.at[pl.ds(block, rows)], loc_sem.at[0])
    copy_cot = pltpu.make_async_copy(cot, cot_v, loc_sem.at[1])
    copy_own = pltpu.make_async_copy(cot.at[pl.ds(tm * share, share)], cot_w.at[tm], loc_sem.at[2])
    copy_feat.start()
    copy_own.start()
    copy_cot.start()

    partners = [dev_bus(-1), dev_bus(1)]
    partners += [dev_q(d) for d in range(1, nq)]
    partners += [dev_y(d) for d in range(1, ny)]
    partners += [dev_z(d) for d in range(1, nz)]
    barrier = pltpu.get_barrier_semaphore()
    for partner in partners:
        pl.semaphore_signal(barrier, inc=1, device_id=partner, device_id_type=MESH)

    side = 16 * steps
    row_id = lax.broadcasted_iota(jnp.int32, (side, side), 0)
    col_id = lax.broadcasted_iota(jnp.int32, (side, side), 1)
    swapped = (row_id % 16) * 16 + row_id // 16
    perm[...] = jnp.where(col_id == swapped, 1.0, 0.0).astype(BF16)

    for i in range(2):
        sums = [jnp.zeros((block, block), F32) for _ in range(4)]
        for k in range(8):
            target = nbr[i, k] - (2 * bus - 1)
            value = coup[i, k].astype(F32)
            for place in range(4):
                weight = jnp.where(target == place, 1.0, 0.0).astype(F32)
                sums[place] = sums[place] + weight * value
        full = jnp.concatenate(sums, axis=1)
        high, low = split(full)
        m_mat[0, pl.ds(i * block, block), :] = high
        m_mat[1, pl.ds(i * block, block), :] = low
    for part in range(2):
        mt_mat[part] = m_mat[part].astype(F32).T.astype(BF16)
    tap_rows = taps[...]
    spectrum = mm(fwd_tab[...], jnp.concatenate([tap_rows, tap_rows], axis=0))
    length = tap_rows.shape[0]
    kr[...] = spectrum[:length]
    ki[...] = spectrum[length:]

    pl.semaphore_wait(barrier, len(partners))

    to_next = remote(feat.at[pl.ds(block, block)], fx.at[pl.ds(0, block)], halo_s.at[0], halo_r.at[0], dev_bus(1))
    to_prev = remote(feat.at[pl.ds(0, block)], fx.at[pl.ds(rows + block, block)], halo_s.at[1], halo_r.at[1], dev_bus(-1))
    to_next.start()
    to_prev.start()
    cot_copies = []
    for d in range(1, nx):
        peer = lax.rem(tm + d, nx)
        cot_copies.append(
            remote(cot.at[pl.ds(peer * share, share)], cot_w.at[tm], cot_s.at[d], cot_r.at[d], dev_x(d))
        )
    for copy in cot_copies:
        copy.start()

    def to_time_major(src, dst, first, pairs):
        def body(pair, carry):
            at = first + pair * 32
            left = src[pl.ds(at, 16)].reshape(side, chans)
            right = src[pl.ds(at + 16, 16)].reshape(side, chans)
            moved = mm(perm[...], jnp.concatenate([left, right], axis=1)).astype(BF16)
            start = pl.multiple_of(at, 16)
            dst[:, pl.ds(start, 16), :] = moved[:, :chans].reshape(steps, 16, chans)
            dst[:, pl.ds(start + 16, 16), :] = moved[:, chans:].reshape(steps, 16, chans)
            return carry

        lax.fori_loop(0, pairs, body, 0)

    copy_feat.wait()
    to_time_major(fx, ft, block, rows // 32)
    to_next.wait()
    to_time_major(fx, ft, 0, block // 32)
    to_prev.wait()
    to_time_major(fx, ft, rows + block, block // 32)

    def forward(pair, carry):
        t = pair * 2
        both = jnp.concatenate([ft[t], ft[t + 1]], axis=1)
        mix = (mm(m_mat[0], both) + mm(m_mat[1], both)).astype(BF16)
        for half in range(2):
            mix_one = mix[:, half * chans : (half + 1) * chans]
            mixed[t + half] = mix_one
            pre = mm(mix_one, wg[...])
            gate = 1.0 / (1.0 + jnp.exp(-pre))
            act_t[t + half] = (pre * gate).astype(BF16)
            slope[t + half] = gate * (1.0 + pre * (1.0 - gate))
        return carry

    lax.fori_loop(0, steps // 2, forward, 0)

    def act_rows(at):
        start = pl.multiple_of(at, 16)
        left = act_t[:, pl.ds(start, 16), :].reshape(side, chans)
        right = act_t[:, pl.ds(start + 16, 16), :].reshape(side, chans)
        moved = mm(perm[...], jnp.concatenate([left, right], axis=1)).astype(BF16)
        return moved[:, :chans].reshape(16, steps, chans), moved[:, chans:].reshape(16, steps, chans)

    act_copies = []
    for d in list(range(1, nx)) + [0]:
        peer = lax.rem(tm + d, nx)
        for piece in range(share // 32):
            at = peer * share + piece * 32
            left, right = act_rows(at)
            if d == 0:
                act_w[tm, pl.ds(piece * 32, 16)] = left
                act_w[tm, pl.ds(piece * 32 + 16, 16)] = right
            else:
                act_b[d, pl.ds(piece * 32, 16)] = left
                act_b[d, pl.ds(piece * 32 + 16, 16)] = right
        if d:
            copy = remote(act_b.at[d], act_w.at[tm], act_s.at[d], act_r.at[d], dev_x(d))
            copy.start()
            act_copies.append(copy)

    copy_own.wait()
    for copy in cot_copies:
        copy.wait()

    group = 4
    lanes = group * chans

    def wide(src, at):
        cols = []
        for b in range(group):
            cols.append(jnp.concatenate([src[j, at + b] for j in range(nx)], axis=0))
        return jnp.concatenate(cols, axis=1)

    def tiled(table):
        return jnp.concatenate([table] * group, axis=1)

    def inverse(real, imag):
        high, low = split(jnp.concatenate([real, imag], axis=0))
        return mm(inv_tab[...], jnp.concatenate([high, low, high], axis=0))

    def backward(step, carry):
        at = step * group
        for j in range(nx):
            cot_rows = cot_w[j, pl.ds(at, group)].reshape(group * steps, chans)
            conv_rows = mm_t(cot_rows, wo[...], 1, 1).astype(BF16)
            gc_w[j] = conv_rows.reshape(group, steps, chans)
        data = wide(gc_w, 0)
        spec = mm(fwd_tab[...], jnp.concatenate([data, data], axis=0))
        g_freq[step] = spec
        gr, gi = spec[:length], spec[length:]
        k_re, k_im = tiled(kr[...]), tiled(ki[...])
        back = inverse(k_re * gr + k_im * gi, k_re * gi - k_im * gr).astype(BF16)
        for b in range(group):
            for j in range(nx):
                grad_w[j, at + b] = back[j * steps : (j + 1) * steps, b * chans : (b + 1) * chans]
        return carry

    lax.fori_loop(0, share // group, backward, 0)

    grad_copies = []
    for d in range(1, nx):
        peer = lax.rem(tm + d, nx)
        copy = remote(grad_w.at[peer], grad_b.at[pl.ds(tm * share, share)], grd_s.at[d], grd_r.at[d], dev_x(d))
        copy.start()
        grad_copies.append(copy)
    grad_b[pl.ds(tm * share, share)] = grad_w[tm]

    for copy in act_copies:
        copy.wait()

    red_b[...] = jnp.zeros_like(red_b)

    def convolve(step, carry):
        tap_re, tap_im = carry
        at = step * group
        data = wide(act_w, at)
        spec = mm(fwd_tab[...], jnp.concatenate([data, data], axis=0))
        ar, ai = spec[:length], spec[length:]
        k_re, k_im = tiled(kr[...]), tiled(ki[...])
        conv = inverse(k_re * ar - k_im * ai, k_re * ai + k_im * ar).astype(BF16)
        conv_rows = jnp.concatenate([conv[:, b * chans : (b + 1) * chans] for b in range(group)], axis=0)
        cot_cols = wide(cot_w, at)
        cot_rows = jnp.concatenate([cot_cols[:, b * chans : (b + 1) * chans] for b in range(group)], axis=0)
        red_b[pl.ds(0, chans), :] += mm_t(conv_rows, cot_rows, 0, 0)
        gr, gi = g_freq[step, pl.ds(0, length), :], g_freq[step, pl.ds(length, length), :]
        p_re = ar * gr + ai * gi
        p_im = ar * gi - ai * gr
        for b in range(group):
            tap_re = tap_re + p_re[:, b * chans : (b + 1) * chans]
            tap_im = tap_im + p_im[:, b * chans : (b + 1) * chans]
        return tap_re, tap_im

    zero = jnp.zeros((length, chans), F32)
    tap_re, tap_im = lax.fori_loop(0, share // group, convolve, (zero, zero))
    red_b[pl.ds(chans, length), :] = inverse(tap_re, tap_im)

    def scatter(red, rs, send, recv):
        size = red.shape[0] // nq
        copies = []
        for d in range(1, nq):
            start = pl.multiple_of(q_at(d) * size, 8)
            copy = remote(red.at[pl.ds(start, size)], rs.at[d], send.at[d], recv.at[d], dev_q(d))
            copy.start()
            copies.append(copy)
        return copies

    def exchange_y(red, rs, copies, buf, send, recv):
        size = red.shape[0] // nq
        for copy in copies:
            copy.wait()
        start = pl.multiple_of(qq * size, 8)
        total = red[pl.ds(start, size), :]
        for d in range(1, nq):
            total = total + rs[d]
        buf[yy] = total
        out = [remote(buf.at[yy], buf.at[yy], send.at[d], recv.at[d], dev_y(d)) for d in range(1, ny)]
        for copy in out:
            copy.start()
        return out

    def exchange_z(last, copies, buf, send, recv):
        for copy in copies:
            copy.wait()
        total = last[0]
        for i in range(1, ny):
            total = total + last[i]
        buf[zz] = total
        out = [remote(buf.at[zz], buf.at[zz], send.at[d], recv.at[d], dev_z(d)) for d in range(1, nz)]
        for copy in out:
            copy.start()
        return out

    def gather(red, last, copies, send, recv):
        size = red.shape[0] // nq
        for copy in copies:
            copy.wait()
        total = last[0]
        for i in range(1, nz):
            total = total + last[i]
        start = pl.multiple_of(qq * size, 8)
        red[pl.ds(start, size), :] = total
        piece = red.at[pl.ds(start, size)]
        out = [remote(piece, piece, send.at[d], recv.at[d], dev_q(d)) for d in range(1, nq)]
        for copy in out:
            copy.start()
        return out

    rs_b_copies = scatter(red_b, rs_b, rsb_s, rsb_r)

    for copy in grad_copies:
        copy.wait()
    to_time_major(grad_b, act_t, 0, rows // 32)
    red_a[...] = jnp.zeros_like(red_a)

    def graph_back(pair, carry):
        t = pair * 2
        rows_two = act_t[pl.ds(t, 2)].reshape(2 * rows, chans).astype(F32)
        slope_two = slope[pl.ds(t, 2)].reshape(2 * rows, chans)
        grad_pre = (rows_two * slope_two).astype(BF16)
        mixed_two = mixed[pl.ds(t, 2)].reshape(2 * rows, chans)
        red_a[...] += mm_t(mixed_two, grad_pre, 0, 0)
        grad_mixed = mm_t(grad_pre, wg[...], 1, 1).astype(BF16)
        both = jnp.concatenate([grad_mixed[:rows], grad_mixed[rows:]], axis=1)
        spread = mm(mt_mat[0], both) + mm(mt_mat[1], both)
        for half in range(2):
            part = spread[:, half * chans : (half + 1) * chans]
            send_prev[t + half] = part[:block].astype(BF16)
            own[t + half] = part[block : block + rows]
            send_next[t + half] = part[block + rows :].astype(BF16)
        return carry

    lax.fori_loop(0, steps // 2, graph_back, 0)
    grad_next = remote(send_next, from_prev, ghalo_s.at[0], ghalo_r.at[0], dev_bus(1))
    grad_prev = remote(send_prev, from_next, ghalo_s.at[1], ghalo_r.at[1], dev_bus(-1))
    grad_next.start()
    grad_prev.start()
    rs_a_copies = scatter(red_a, rs_a, rsa_s, rsa_r)
    y_b_copies = exchange_y(red_b, rs_b, rs_b_copies, y_b, yb_s, yb_r)
    y_a_copies = exchange_y(red_a, rs_a, rs_a_copies, y_a, ya_s, ya_r)
    z_b_copies = exchange_z(y_b, y_b_copies, z_b, zb_s, zb_r)
    z_a_copies = exchange_z(y_a, y_a_copies, z_a, za_s, za_r)

    grad_next.wait()
    grad_prev.wait()
    copy_cot.wait()

    def finish(piece, carry):
        at = pl.multiple_of(piece * 16, 16)
        for half, other in ((0, from_prev), (1, from_next)):
            first = pl.multiple_of(half * block + at, 16)
            total = own[:, pl.ds(first, 16), :] + other[:, pl.ds(at, 16), :].astype(F32)
            high, low = split(total.reshape(side, chans))
            both = mm(perm[...], jnp.concatenate([high, low], axis=1))
            moved = both[:, :chans] + both[:, chans:]
            base = cot_v[pl.ds(first, 16)].reshape(side, chans).astype(F32)
            out_v[pl.ds(first, 16)] = (moved + base).astype(BF16).reshape(16, steps, chans)
        return carry

    lax.fori_loop(0, block // 16, finish, 0)
    copy_out = pltpu.make_async_copy(out_v, grad_feat, out_sem)
    copy_out.start()

    ag_b_copies = gather(sum_b, z_b, z_b_copies, agb_s, agb_r)
    ag_a_copies = gather(sum_a, z_a, z_a_copies, aga_s, aga_r)
    for copy in ag_b_copies:
        copy.wait()
    grad_out[...] = sum_b[pl.ds(0, chans), :] * scale
    grad_taps[...] = sum_b[pl.ds(chans, length), :] * scale
    for copy in ag_a_copies:
        copy.wait()
    grad_graph[...] = sum_a[...] * scale
    copy_out.wait()


def shards(sizes, features, couplings, neighbors, w_graph, kernel_taps, w_out, cotangent):
    nbus, nx, ny, nz, scale = sizes
    rows, steps, chans = features.shape
    length = kernel_taps.shape[0]
    block = couplings.shape[2]
    share = rows // nx
    nq = nx * CORES
    group = 4
    fwd_tab, inv_tab = dft_tables(length)
    size_a = chans // nq
    size_b = (chans + length) // nq
    vmem = pltpu.VMEM
    dma = pltpu.SemaphoreType.DMA
    in_vmem = pl.BlockSpec(memory_space=pltpu.VMEM)
    in_any = pl.BlockSpec(memory_space=pl.ANY)
    scratch = [
        vmem((rows + 2 * block, steps, chans), BF16),
        vmem((steps, rows + 2 * block, chans), BF16),
        vmem((16 * steps, 16 * steps), BF16),
        vmem((2, rows, rows + 2 * block), BF16),
        vmem((2, rows + 2 * block, rows), BF16),
        vmem((steps, rows, chans), BF16),
        vmem((steps, rows, chans), F32),
        vmem((steps, rows, chans), BF16),
        vmem((nx, share, steps, chans), BF16),
        vmem((nx, share, steps, chans), BF16),
        vmem((rows, steps, chans), BF16),
        vmem((nx, share, steps, chans), BF16),
        vmem((nx, group, steps, chans), BF16),
        vmem((share // group, 2 * length, group * chans), F32),
        vmem((length, chans), F32),
        vmem((length, chans), F32),
        vmem((nx, share, steps, chans), BF16),
        vmem((rows, steps, chans), BF16),
        vmem((steps, rows, chans), F32),
        vmem((steps, block, chans), BF16),
        vmem((steps, block, chans), BF16),
        vmem((steps, block, chans), BF16),
        vmem((steps, block, chans), BF16),
        vmem((rows, steps, chans), BF16),
        vmem((chans, chans), F32),
        vmem((nq, size_a, chans), F32),
        vmem((ny, size_a, chans), F32),
        vmem((nz, size_a, chans), F32),
        vmem((chans, chans), F32),
        vmem((chans + length, chans), F32),
        vmem((nq, size_b, chans), F32),
        vmem((ny, size_b, chans), F32),
        vmem((nz, size_b, chans), F32),
        vmem((chans + length, chans), F32),
        dma((3,)),
        dma,
    ]
    for count in (2, nx, nx, nx, 2, nq, nq, ny, ny, nz, nz, nq, nq):
        scratch += [dma((count,)), dma((count,))]
    return pl.pallas_call(
        functools.partial(kernel, sizes),
        out_shape=(
            jax.ShapeDtypeStruct(features.shape, BF16),
            jax.ShapeDtypeStruct((chans, chans), F32),
            jax.ShapeDtypeStruct((chans, chans), F32),
            jax.ShapeDtypeStruct((length, chans), F32),
        ),
        in_specs=[in_any, in_any, in_vmem, pl.BlockSpec(memory_space=pltpu.SMEM)] + [in_vmem] * 5,
        out_specs=(in_any, in_vmem, in_vmem, in_vmem),
        scratch_shapes=scratch,
        compiler_params=pltpu.CompilerParams(
            collective_id=0, has_side_effects=True, vmem_limit_bytes=40 * 1024 * 1024
        ),
    )(features, cotangent, couplings, neighbors, w_graph, kernel_taps, w_out, jnp.asarray(fwd_tab), jnp.asarray(inv_tab))


def solution(mesh):
    nbus, nx = mesh.shape["bus"], mesh.shape["tm"]
    nz = nbus // (CORES * CHIPS_Y)

    def step(features, couplings, neighbors, w_graph, kernel_taps, w_out, cotangent):
        total_rows = nbus * features.shape[0] * features.shape[1] * nx
        sizes = (nbus, nx, CHIPS_Y, nz, 1.0 / math.sqrt(total_rows))
        return shards(sizes, features, couplings, neighbors, w_graph, kernel_taps, w_out, cotangent)

    return jax.shard_map(
        step,
        mesh=mesh,
        in_specs=(
            P("bus", "tm", None),
            P("bus", None, None, None),
            P("bus", None),
            P(),
            P(),
            P(),
            P("bus", "tm", None),
        ),
        out_specs=(P("bus", "tm", None), P(), P(), P()),
        check_vma=False,
    )
```

time: 481 us -> 66.6 us (0.14)
  waiting for transfers between devices: 240 us -> 0 us
  blocking collectives: 83.5 us -> 0 us
  Pallas kernels: 0 us -> 55.2 us
  local copies, waits for them, and re-layouts: 58.9 us -> 10.2 us
  other arithmetic: 29.2 us -> 0 us
  matrix products: 26.7 us -> 0 us
  starting transfers between devices: 26.2 us -> 0 us
  between operations: 14.5 us -> 0.66 us
    psum x1 -> x0, waiting for transfers between devices: 240 us -> none  [shards(): summed = lax.psum((part_graph, part_out, part_taps), ('bus', 'tm'))]
    psum x1 -> x0, blocking collectives: 83.5 us -> none  [shards(): summed = lax.psum((part_graph, part_out, part_taps), ('bus', 'tm'))]
    pallas_call x0 -> x1, Pallas kernels: none -> 55.2 us  [shards(): pl.pallas_call(functools.partial(kernel, sizes), out_shape=(jax.ShapeDtyp...]
    dot_general x17 -> x0, matrix products: 26.7 us -> none  [the longest x8 10.6 us: shards(): jnp.einsum('iab,ian->ibn', couplings[:, slot_index], grad_mixed, preferre...]
    gather x3 -> x0, local copies, waits for them, and re-layouts: 18.7 us -> none  [the longest x2 15.9 us: toeplitz_table(): picked = jnp.take(kernel_taps.T, jnp.clip(lagged, 0, length - 1), axis=1)]
    scatter-add x8 -> x0, other arithmetic: 17.4 us -> none  [shards(): spread = spread.at[position[:, slot_index]].add(slot_term)]
    ppermute x4 -> x0, starting transfers between devices: 13.6 us -> none  [the longest x2 6.99 us: shifted(): lax.ppermute(value, axis, [(source, source + steps) for source in range(f...]
    all_to_all x3 -> x0, starting transfers between devices: 12.5 us -> none  [the longest x1 4.32 us: shards(): lax.all_to_all(grad_act, 'tm', split_axis=1, concat_axis=0, tiled=True)]
  transfers between devices with their start and end apart: 8 -> 0, of which waited for: 2 -> 0; matrix products, arithmetic and copies ran while one was open for 16% -> 0% of each run, Pallas kernels for 0% -> 0%
where the time goes in v1:
time: 66.6 us; the launch traced here: 66 us
  Pallas kernels  55.2 us (83%)
  local copies, waits for them, and re-layouts  10.2 us (15%)
    pallas_call x1, Pallas kernels, shards(): pl.pallas_call(functools.partial(kernel, sizes), out_shape=(jax.ShapeDtyp...  55.2 us
    unnamed x22, local copies, waits for them, and re-layouts  10.2 us

profile of v1, /device:TPU:1, one launch (start us, length us, event | category | flops | bytes accessed | tf_op | source)
XLA Modules:
  0.0 66.0 jit_solution(9001240691465359857)
XLA Ops:
  0.6 0.0 copy-start
  0.6 1.0 %copy-done = bf16[128,16,128]{2,1,0:T(8,128)(2,1)S(1)} copy-done((bf16[128,16,128]{2,1,0:T(8,128)(2,1)S(1)}, bf16[128,16,128]{2,1,0:T(8,128)(2,1)}, u32[]{:S(2)}) %copy-start) | copy-done | bytes 524312
  1.7 0.0 copy-start.1
  1.7 1.0 %copy-done.1 = bf16[128,16,128]{2,1,0:T(8,128)(2,1)S(1)} copy-done((bf16[128,16,128]{2,1,0:T(8,128)(2,1)S(1)}, bf16[128,16,128]{2,1,0:T(8,128)(2,1)}, u32[]{:S(2)}) %copy-start.1) | copy-done | bytes 524312
  2.7 0.0 copy-start.2
  2.7 0.9 %copy-done.2 = bf16[2,8,64,64]{3,2,1,0:T(8,128)(2,1)S(1)} copy-done((bf16[2,8,64,64]{3,2,1,0:T(8,128)(2,1)S(1)}, bf16[2,8,64,64]{3,2,1,0:T(8,128)(2,1)}, u32[]{:S(2)}) %copy-start.2) | copy-done | bytes 131096
  3.7 0.0 copy-start.3
  3.7 0.8 %copy-done.3 = bf16[64,384]{1,0:T(8,128)(2,1)S(1)} copy-done((bf16[64,384]{1,0:T(8,128)(2,1)S(1)}, bf16[64,384]{1,0:T(8,128)(2,1)}, u32[]{:S(2)}) %copy-start.3) | copy-done | bytes 49176
  4.5 0.0 copy-start.4
  4.5 0.8 %copy-done.4 = bf16[128,128]{1,0:T(8,128)(2,1)S(1)} copy-done((bf16[128,128]{1,0:T(8,128)(2,1)S(1)}, bf16[128,128]{1,0:T(8,128)(2,1)}, u32[]{:S(2)}) %copy-start.4) | copy-done | bytes 32792
  5.2 0.0 copy-start.5
  5.2 0.8 %copy-done.5 = bf16[128,128]{1,0:T(8,128)(2,1)S(1)} copy-done((bf16[128,128]{1,0:T(8,128)(2,1)S(1)}, bf16[128,128]{1,0:T(8,128)(2,1)}, u32[]{:S(2)}) %copy-start.5) | copy-done | bytes 32792
  6.0 0.0 copy-start.6
  6.0 0.8 %copy-done.6 = bf16[128,128]{1,0:T(8,128)(2,1)S(1)} copy-done((bf16[128,128]{1,0:T(8,128)(2,1)S(1)}, bf16[128,128]{1,0:T(8,128)(2,1)}, u32[]{:S(2)}) %copy-start.6) | copy-done | bytes 32792
  6.7 0.0 copy-start.7
  6.7 0.7 %copy-done.7 = bf16[64,128]{1,0:T(8,128)(2,1)S(1)} copy-done((bf16[64,128]{1,0:T(8,128)(2,1)S(1)}, bf16[64,128]{1,0:T(8,128)(2,1)}, u32[]{:S(2)}) %copy-start.7) | copy-done | bytes 16408
  7.5 0.0 copy-start.8
  7.5 0.7 %copy-done.8 = s32[2,8]{1,0:T(2,128)S(1)} copy-done((s32[2,8]{1,0:T(2,128)S(1)}, s32[2,8]{1,0:T(2,128)}, u32[]{:S(2)}) %copy-start.8) | copy-done | bytes 88
  8.1 55.2 %shard_map.120 = (bf16[128,16,128]{2,1,0:T(8,128)(2,1)S(1)}, f32[128,128]{1,0:T(8,128)S(1)}, f32[128,128]{1,0:T(8,128)S(1)}, f32[64,128]{1,0:T(8,128)S(1)}) custom-call(bf16[128,16,128]{2,1,0:T(8,128)(2,1)S(1)} %copy-done, bf16[128,16,128]{2,1,0:T(8,128)(2,1)S(1)} %copy-done.1, bf16[2,8,64,64]{3,2,1,0:T(8,128)(2,1)S(1)} %copy-done.2, s32[2,8]{1,0:T(2,128)S(1)} %copy-done.8, ...), custom_call_target="tpu_custom_call" | custom-call | tf_op jit(solution)/shard_map/pallas_call | solution.py:531
  63.4 0.8 %copy.17 = bf16[128,16,128]{2,1,0:T(8,128)(2,1)} copy(bf16[128,16,128]{2,1,0:T(8,128)(2,1)S(1)} %get-tuple-element.8) | data formatting | bytes 1048576
  64.2 0.6 copy.18
  64.8 0.6 copy.19
  65.4 0.6 copy.20
Async XLA Ops:
  0.6 1.0 %copy-start = (bf16[128,16,128]{2,1,0:T(8,128)(2,1)S(1)}, bf16[128,16,128]{2,1,0:T(8,128)(2,1)}, u32[]{:S(2)}) copy-start(bf16[128,16,128]{2,1,0:T(8,128)(2,1)} %feat.1) | copy-start | bytes 1572868
  1.7 1.0 %copy-start.1 = (bf16[128,16,128]{2,1,0:T(8,128)(2,1)S(1)}, bf16[128,16,128]{2,1,0:T(8,128)(2,1)}, u32[]{:S(2)}) copy-start(bf16[128,16,128]{2,1,0:T(8,128)(2,1)} %cot.1) | copy-start | bytes 1572868
  2.7 0.9 %copy-start.2 = (bf16[2,8,64,64]{3,2,1,0:T(8,128)(2,1)S(1)}, bf16[2,8,64,64]{3,2,1,0:T(8,128)(2,1)}, u32[]{:S(2)}) copy-start(bf16[2,8,64,64]{3,2,1,0:T(8,128)(2,1)} %coup.1) | copy-start | bytes 393220
  3.7 0.8 %copy-start.3 = (bf16[64,384]{1,0:T(8,128)(2,1)S(1)}, bf16[64,384]{1,0:T(8,128)(2,1)}, u32[]{:S(2)}) copy-start(bf16[64,384]{1,0:T(8,128)(2,1)} %constant.5.clone.inv_tab) | copy-start | bytes 147460
  4.5 0.8 %copy-start.4 = (bf16[128,128]{1,0:T(8,128)(2,1)S(1)}, bf16[128,128]{1,0:T(8,128)(2,1)}, u32[]{:S(2)}) copy-start(bf16[128,128]{1,0:T(8,128)(2,1)} %wg.1) | copy-start | bytes 98308
  5.2 0.8 %copy-start.5 = (bf16[128,128]{1,0:T(8,128)(2,1)S(1)}, bf16[128,128]{1,0:T(8,128)(2,1)}, u32[]{:S(2)}) copy-start(bf16[128,128]{1,0:T(8,128)(2,1)} %wo.1) | copy-start | bytes 98308
  6.0 0.8 %copy-start.6 = (bf16[128,128]{1,0:T(8,128)(2,1)S(1)}, bf16[128,128]{1,0:T(8,128)(2,1)}, u32[]{:S(2)}) copy-start(bf16[128,128]{1,0:T(8,128)(2,1)} %constant.4.clone.fwd_tab) | copy-start | bytes 98308
  6.7 0.7 %copy-start.7 = (bf16[64,128]{1,0:T(8,128)(2,1)S(1)}, bf16[64,128]{1,0:T(8,128)(2,1)}, u32[]{:S(2)}) copy-start(bf16[64,128]{1,0:T(8,128)(2,1)} %taps.1) | copy-start | bytes 49156
  7.5 0.7 %copy-start.8 = (s32[2,8]{1,0:T(2,128)S(1)}, s32[2,8]{1,0:T(2,128)}, u32[]{:S(2)}) copy-start(s32[2,8]{1,0:T(2,128)} %nbr.1) | copy-start | bytes 196

commit v2 on v1

--- a/solution.py
+++ b/solution.py
@@ -54,6 +54,17 @@
     sizes,
     feat,
     cot,
+    coup_h,
+    nbr_h,
+    wg_h,
+    taps_h,
+    wo_h,
+    fwd_h,
+    inv_h,
+    grad_feat,
+    grad_graph,
+    grad_out,
+    grad_taps,
     coup,
     nbr,
     wg,
@@ -61,10 +72,6 @@
     wo,
     fwd_tab,
     inv_tab,
-    grad_feat,
-    grad_graph,
-    grad_out,
-    grad_taps,
     fx,
     ft,
     perm,
@@ -88,7 +95,6 @@
     send_next,
     from_prev,
     from_next,
-    out_v,
     red_a,
     rs_a,
     y_a,
@@ -100,7 +106,6 @@
     z_b,
     sum_b,
     loc_sem,
-    out_sem,
     halo_s,
     halo_r,
     cot_s,
@@ -167,6 +172,10 @@
     copy_feat = pltpu.make_async_copy(feat, fx.at[pl.ds(block, rows)], loc_sem.at[0])
     copy_cot = pltpu.make_async_copy(cot, cot_v, loc_sem.at[1])
     copy_own = pltpu.make_async_copy(cot.at[pl.ds(tm * share, share)], cot_w.at[tm], loc_sem.at[2])
+    small = [(nbr_h, nbr), (coup_h, coup), (taps_h, taps), (fwd_h, fwd_tab), (wg_h, wg), (wo_h, wo), (inv_h, inv_tab)]
+    small_copies = [pltpu.make_async_copy(src, dst, loc_sem.at[3 + i]) for i, (src, dst) in enumerate(small)]
+    for copy in small_copies:
+        copy.start()
     copy_feat.start()
     copy_own.start()
     copy_cot.start()
@@ -185,6 +194,8 @@
     swapped = (row_id % 16) * 16 + row_id // 16
     perm[...] = jnp.where(col_id == swapped, 1.0, 0.0).astype(BF16)
 
+    for copy in small_copies:
+        copy.wait()
     for i in range(2):
         sums = [jnp.zeros((block, block), F32) for _ in range(4)]
         for k in range(8):
@@ -454,12 +465,10 @@
             both = mm(perm[...], jnp.concatenate([high, low], axis=1))
             moved = both[:, :chans] + both[:, chans:]
             base = cot_v[pl.ds(first, 16)].reshape(side, chans).astype(F32)
-            out_v[pl.ds(first, 16)] = (moved + base).astype(BF16).reshape(16, steps, chans)
+            grad_feat[pl.ds(first, 16)] = (moved + base).astype(BF16).reshape(16, steps, chans)
         return carry
 
     lax.fori_loop(0, block // 16, finish, 0)
-    copy_out = pltpu.make_async_copy(out_v, grad_feat, out_sem)
-    copy_out.start()
 
     ag_b_copies = gather(sum_b, z_b, z_b_copies, agb_s, agb_r)
     ag_a_copies = gather(sum_a, z_a, z_a_copies, aga_s, aga_r)
@@ -470,7 +479,6 @@
     for copy in ag_a_copies:
         copy.wait()
     grad_graph[...] = sum_a[...] * scale
-    copy_out.wait()
 
 
 def shards(sizes, features, couplings, neighbors, w_graph, kernel_taps, w_out, cotangent):
@@ -488,7 +496,15 @@
     dma = pltpu.SemaphoreType.DMA
     in_vmem = pl.BlockSpec(memory_space=pltpu.VMEM)
     in_any = pl.BlockSpec(memory_space=pl.ANY)
+    in_hbm = pl.BlockSpec(memory_space=pltpu.HBM)
     scratch = [
+        vmem(couplings.shape, BF16),
+        pltpu.SMEM(neighbors.shape, jnp.int32),
+        vmem(w_graph.shape, BF16),
+        vmem(kernel_taps.shape, BF16),
+        vmem(w_out.shape, BF16),
+        vmem(fwd_tab.shape, BF16),
+        vmem(inv_tab.shape, BF16),
         vmem((rows + 2 * block, steps, chans), BF16),
         vmem((steps, rows + 2 * block, chans), BF16),
         vmem((16 * steps, 16 * steps), BF16),
@@ -512,7 +528,6 @@
         vmem((steps, block, chans), BF16),
         vmem((steps, block, chans), BF16),
         vmem((steps, block, chans), BF16),
-        vmem((rows, steps, chans), BF16),
         vmem((chans, chans), F32),
         vmem((nq, size_a, chans), F32),
         vmem((ny, size_a, chans), F32),
@@ -523,8 +538,7 @@
         vmem((ny, size_b, chans), F32),
         vmem((nz, size_b, chans), F32),
         vmem((chans + length, chans), F32),
-        dma((3,)),
-        dma,
+        dma((10,)),
     ]
     for count in (2, nx, nx, nx, 2, nq, nq, ny, ny, nz, nz, nq, nq):
         scratch += [dma((count,)), dma((count,))]
@@ -536,11 +550,11 @@
             jax.ShapeDtypeStruct((chans, chans), F32),
             jax.ShapeDtypeStruct((length, chans), F32),
         ),
-        in_specs=[in_any, in_any, in_vmem, pl.BlockSpec(memory_space=pltpu.SMEM)] + [in_vmem] * 5,
-        out_specs=(in_any, in_vmem, in_vmem, in_vmem),
+        in_specs=[in_hbm] * 9,
+        out_specs=(in_vmem, in_vmem, in_vmem, in_vmem),
         scratch_shapes=scratch,
         compiler_params=pltpu.CompilerParams(
-            collective_id=0, has_side_effects=True, vmem_limit_bytes=40 * 1024 * 1024
+            collective_id=0, has_side_effects=True, vmem_limit_bytes=67043328
         ),
     )(features, cotangent, couplings, neighbors, w_graph, kernel_taps, w_out, jnp.asarray(fwd_tab), jnp.asarray(inv_tab))
 

time: 66.6 us -> 60.7 us (0.911)
  local copies, waits for them, and re-layouts: 10.2 us -> 4.14 us
    unnamed x22 -> x10, local copies, waits for them, and re-layouts: 10.2 us -> 4.14 us
where the time goes in v2:
time: 60.7 us; the launch traced here: 60.5 us
  Pallas kernels  55.7 us (92%)
  local copies, waits for them, and re-layouts  4.14 us (7%)
  between operations  0.65 us (1%)
    pallas_call x1, Pallas kernels, shards(): pl.pallas_call(functools.partial(kernel, sizes), out_shape=(jax.ShapeDtyp...  55.7 us
    unnamed x10, local copies, waits for them, and re-layouts  4.14 us

profile of v2, /device:TPU:1, one launch (start us, length us, event | category | flops | bytes accessed | tf_op | source)
XLA Modules:
  0.0 60.5 jit_solution(18071801516380207902)
XLA Ops:
  0.6 55.7 %shard_map.120 = (bf16[128,16,128]{2,1,0:T(8,128)(2,1)}, f32[128,128]{1,0:T(8,128)}, f32[128,128]{1,0:T(8,128)}, f32[64,128]{1,0:T(8,128)}) custom-call(bf16[128,16,128]{2,1,0:T(8,128)(2,1)} %feat.1, bf16[128,16,128]{2,1,0:T(8,128)(2,1)} %cot.1, bf16[2,8,64,64]{3,2,1,0:T(8,128)(2,1)} %coup_h.1, s32[2,8]{1,0:T(2,128)} %nbr_h.1, bf16[128,128]{1,0:T(8,128)(2,1)} %wg_h.1, ...), custom_call_target="tpu_custom_call" | custom-call | tf_op jit(solution)/shard_map/pallas_call | solution.py:545
  56.3 0.0 copy-start.1
  56.3 1.9 %copy.17 = bf16[128,16,128]{2,1,0:T(8,128)(2,1)} copy(bf16[128,16,128]{2,1,0:T(8,128)(2,1)} %get-tuple-element.8) | data formatting | bytes 1048576
  58.2 0.0 copy-done.1
  58.2 0.0 copy-start
  58.2 0.6 %copy.18 = f32[128,128]{1,0:T(8,128)} copy(f32[128,128]{1,0:T(8,128)S(1)} %copy-done.1) | data formatting | bytes 131072
  58.9 0.2 copy-done
  59.1 0.0 copy-start.2
  59.1 0.6 %copy.19 = f32[128,128]{1,0:T(8,128)} copy(f32[128,128]{1,0:T(8,128)S(1)} %copy-done) | data formatting | bytes 131072
  59.7 0.1 copy-done.2
  59.9 0.6 %copy.20 = f32[64,128]{1,0:T(8,128)} copy(f32[64,128]{1,0:T(8,128)S(1)} %copy-done.2) | data formatting | bytes 65536
Async XLA Ops:
  56.3 1.9 %copy-start.1 = (f32[128,128]{1,0:T(8,128)S(1)}, f32[128,128]{1,0:T(8,128)}, u32[]{:S(2)}) copy-start(f32[128,128]{1,0:T(8,128)} %get-tuple-element.9) | copy-start | bytes 196612
  58.2 0.9 %copy-start = (f32[128,128]{1,0:T(8,128)S(1)}, f32[128,128]{1,0:T(8,128)}, u32[]{:S(2)}) copy-start(f32[128,128]{1,0:T(8,128)} %get-tuple-element.10) | copy-start | bytes 196612
  59.1 0.8 %copy-start.2 = (f32[64,128]{1,0:T(8,128)S(1)}, f32[64,128]{1,0:T(8,128)}, u32[]{:S(2)}) copy-start(f32[64,128]{1,0:T(8,128)} %get-tuple-element.11) | copy-start | bytes 98308

commit v3 on v2

--- a/solution.py
+++ b/solution.py
@@ -481,6 +481,15 @@
     grad_graph[...] = sum_a[...] * scale
 
 
+def store(*refs):
+    sem = refs[8]
+    copies = [pltpu.make_async_copy(src, dst, sem.at[i]) for i, (src, dst) in enumerate(zip(refs[:4], refs[4:8]))]
+    for copy in copies:
+        copy.start()
+    for copy in copies:
+        copy.wait()
+
+
 def shards(sizes, features, couplings, neighbors, w_graph, kernel_taps, w_out, cotangent):
     nbus, nx, ny, nz, scale = sizes
     rows, steps, chans = features.shape
@@ -542,7 +551,7 @@
     ]
     for count in (2, nx, nx, nx, 2, nq, nq, ny, ny, nz, nz, nq, nq):
         scratch += [dma((count,)), dma((count,))]
-    return pl.pallas_call(
+    results = pl.pallas_call(
         functools.partial(kernel, sizes),
         out_shape=(
             jax.ShapeDtypeStruct(features.shape, BF16),
@@ -557,6 +566,13 @@
             collective_id=0, has_side_effects=True, vmem_limit_bytes=67043328
         ),
     )(features, cotangent, couplings, neighbors, w_graph, kernel_taps, w_out, jnp.asarray(fwd_tab), jnp.asarray(inv_tab))
+    return pl.pallas_call(
+        store,
+        out_shape=tuple(jax.ShapeDtypeStruct(r.shape, r.dtype) for r in results),
+        in_specs=[in_vmem] * 4,
+        out_specs=(in_hbm,) * 4,
+        scratch_shapes=[dma((4,))],
+    )(*results)
 
 
 def solution(mesh):

time: 60.7 us -> 58.4 us (0.962)
  local copies, waits for them, and re-layouts: 4.14 us -> 0 us
  Pallas kernels: 55.7 us -> 57.6 us
    unnamed x10 -> x0, local copies, waits for them, and re-layouts: 4.14 us -> none
    pallas_call x0 -> x1, Pallas kernels: none -> 1.95 us  [shards(): pl.pallas_call(store, out_shape=tuple((jax.ShapeDtypeStruct(r.shape, r.dt...]
where the time goes in v3:
time: 58.4 us; the launch traced here: 58.3 us
  Pallas kernels  57.6 us (99%)
  between operations  0.64 us (1%)
    pallas_call x1, Pallas kernels, shards(): pl.pallas_call(functools.partial(kernel, sizes), out_shape=(jax.ShapeDtyp...  55.7 us
    pallas_call x1, Pallas kernels, shards(): pl.pallas_call(store, out_shape=tuple((jax.ShapeDtypeStruct(r.shape, r.dt...  1.95 us

profile of v3, /device:TPU:1, one launch (start us, length us, event | category | flops | bytes accessed | tf_op | source)
XLA Modules:
  0.0 58.3 jit_solution(1789009876469844192)
XLA Ops:
  0.6 55.7 %shard_map.120 = (bf16[128,16,128]{2,1,0:T(8,128)(2,1)}, f32[128,128]{1,0:T(8,128)}, f32[128,128]{1,0:T(8,128)}, f32[64,128]{1,0:T(8,128)}) custom-call(bf16[128,16,128]{2,1,0:T(8,128)(2,1)} %feat.1, bf16[128,16,128]{2,1,0:T(8,128)(2,1)} %cot.1, bf16[2,8,64,64]{3,2,1,0:T(8,128)(2,1)} %coup_h.1, s32[2,8]{1,0:T(2,128)} %nbr_h.1, bf16[128,128]{1,0:T(8,128)(2,1)} %wg_h.1, ...), custom_call_target="tpu_custom_call" | custom-call | tf_op jit(solution)/shard_map/pallas_call | solution.py:554
  56.3 1.9 %shard_map.121 = (bf16[128,16,128]{2,1,0:T(8,128)(2,1)}, f32[128,128]{1,0:T(8,128)}, f32[128,128]{1,0:T(8,128)}, f32[64,128]{1,0:T(8,128)}) custom-call(bf16[128,16,128]{2,1,0:T(8,128)(2,1)} %get-tuple-element.8.refs_0_, f32[128,128]{1,0:T(8,128)} %get-tuple-element.9.refs_1_, f32[128,128]{1,0:T(8,128)} %get-tuple-element.10.refs_2_, ...), custom_call_target="tpu_custom_call" | custom-call | tf_op jit(solution)/shard_map/pallas_call | solution.py:569
